TPU v7x, 32 devices: a whole 2x2x4 slice. The times are simulated.
32 devices in a mesh: seq: 8 (over z, y), tp: 4 (over x, core).
Axes of the slice: x: 2, y: 2, z: 4, core: 2. Of those that a mesh axis runs over, the one named last changes fastest.
Arguments:
- x_in: bfloat16 [1024, 8192], P('seq', 'tp'), may hold values from -6 to 6
- gate_in: bfloat16 [1024, 8192], P('seq', 'tp'), may hold values from -6 to 6
- conv_weight: float32 [4, 8192], P(None, 'tp'), may hold values from -3 to 3
- conv_bias: float32 [8192], P('tp'), may hold values from -0.5 to 0.5
- x_weight: bfloat16 [8192, 544], P('tp'), may hold values from -0.0625 to 0.0625
- dt_weight: bfloat16 [512, 8192], P(None, 'tp'), may hold values from -0.25 to 0.25
- dt_bias: float32 [8192], P('tp'), may hold values from -5 to -2.5
- decay_rate: float32 [8192, 16], P('tp'), may hold values from 0 to 4
- skip_gain: float32 [8192], P('tp'), may hold values from 0.5 to 1.5
- out_weight: bfloat16 [8192, 4096], P('tp'), may hold values from -0.0625 to 0.0625
- residual_in: bfloat16 [1024, 4096], P(('seq', 'tp')), may hold values from -36 to 36
- norm_gain: float32 [4096], replicated, may hold values from 0.1 to 1.9
- expert_ids: int32 [1024, 2], P(('seq', 'tp')), may hold values from 0 to 7, all different within a row; in each aligned block of 32 rows (0 to 31, 32 to 63, ...) at most 12 rows name the same one
- gate_prob: float32 [1024, 2], P(('seq', 'tp')), may hold values from 0.1 to 1
- up_weight: bfloat16 [4096, 98304], P(None, ('seq', 'tp')), may hold values from -0.09375 to 0.09375
- down_weight: bfloat16 [98304, 4096], P(('seq', 'tp')), may hold values from -0.0546875 to 0.0546875
Outputs:
- mixer_out: bfloat16 [1024, 4096], P(('seq', 'tp'))
- layer_out: bfloat16 [1024, 4096], P(('seq', 'tp'))
Inputs may be any that keep to these rules, and one draw needn't show every extreme that they name: `expert_ids`: each row names two different experts. In each device's aligned block of 32 rows no expert is named by more than 12 rows, a bound that some block reaches.
All inputs are finite; a program needn't handle non-finite values.
Results may differ from a plain program's by a relative error of at most 0.007.
Values may be sent and summed in bfloat16 or wider, within the bound.
A program may use at most 192 MiB of HBM per device.

v0:
```python
import jax
import jax.numpy as jnp
from jax import lax
from jax.sharding import PartitionSpec as P

STATE = 16
DTRANK = 512
EXPERTS = 8


def shifted(value, axis, steps):
    count = lax.axis_size(axis)
    initial, last = (max(0, -steps), min(count, count - steps))
    return lax.ppermute(value, axis, [(source, source + steps) for source in range(initial, last)])


def prefix(part, axis, combine, identity):
    place = lax.axis_index(axis)
    gathered = jax.tree.map(lambda a: lax.all_gather(a, axis), part)
    state = jax.tree.map(lambda a, e: jnp.zeros_like(a) + jnp.asarray(e, a.dtype), part, identity)

    def one(hop, state):
        return combine(
            state, jax.tree.map(lambda a: lax.dynamic_index_in_dim(a, hop, 0, False), gathered)
        )

    return lax.fori_loop(0, place, one, state)


def chain_join(earlier, later):
    return (earlier[0] * later[0], later[0] * earlier[1] + later[1])


def recur_blocks(start_state, step_cols, drive_cols, entry_cols, readout_cols, negative_rate):

    def advance(carried, columns):
        step_row, drive_row, entry_row, readout_row = columns
        carried = (
            jnp.exp(step_row[:, None, :] * negative_rate[None]) * carried
            + entry_row[:, :, None] * drive_row[:, None, :]
        )
        return (carried, jnp.sum(readout_row[:, :, None] * carried, axis=1))

    return lax.scan(advance, start_state, (step_cols, drive_cols, entry_cols, readout_cols))


def by_position(values, blocks, span):
    return values.reshape(blocks, span, values.shape[1]).transpose(1, 0, 2)


def expert_share(arrived_flat, up_weight, down_weight):
    hidden = jax.nn.silu(
        jnp.dot(arrived_flat, up_weight, preferred_element_type=jnp.float32)
    ).astype(jnp.bfloat16)
    return jnp.dot(hidden, down_weight, preferred_element_type=jnp.float32).astype(jnp.bfloat16)


def per_device(
    x_in,
    gate_in,
    conv_weight,
    conv_bias,
    x_weight,
    dt_weight,
    dt_bias,
    decay_rate,
    skip_gain,
    out_weight,
    residual_in,
    norm_gain,
    expert_ids,
    gate_prob,
    up_weight,
    down_weight,
):
    tokens, channels = x_in.shape
    width = out_weight.shape[1]
    reach = conv_weight.shape[0] - 1
    rim_rows = shifted(x_in[tokens - reach :], "seq", 1)
    padded = jnp.concatenate([rim_rows, x_in], axis=0).astype(jnp.float32)
    conv_out = conv_bias[None, :] + sum(
        (
            conv_weight[offset][None, :] * padded[offset : offset + tokens]
            for offset in range(reach + 1)
        )
    )
    inner = jax.nn.silu(conv_out).astype(jnp.bfloat16)
    projected = lax.psum(jnp.dot(inner, x_weight, preferred_element_type=jnp.float32), "tp")
    dt_low = projected[:, :DTRANK].astype(jnp.bfloat16)
    entry_rows = projected[:, DTRANK : DTRANK + STATE]
    readout_rows = projected[:, DTRANK + STATE :]
    step_size = jax.nn.softplus(
        jnp.dot(dt_low, dt_weight, preferred_element_type=jnp.float32) + dt_bias[None, :]
    )
    drive = step_size * inner.astype(jnp.float32)
    negative_rate = -decay_rate.T
    span = 16
    blocks = tokens // span
    step_cols = by_position(step_size, blocks, span)
    drive_cols = by_position(drive, blocks, span)
    entry_cols = by_position(entry_rows, blocks, span)
    readout_cols = by_position(readout_rows, blocks, span)
    zero_blocks = jnp.zeros((blocks, STATE, channels), jnp.float32)
    block_ends, local_out = recur_blocks(
        zero_blocks, step_cols, drive_cols, entry_cols, readout_cols, negative_rate
    )
    block_decay = jnp.exp(negative_rate[None] * jnp.sum(step_cols, axis=0)[:, None, :])
    decay_through, state_through = lax.associative_scan(
        chain_join, (block_decay, block_ends), axis=0
    )
    ones_state = jnp.ones((STATE, channels), jnp.float32)
    zeros_state = jnp.zeros((STATE, channels), jnp.float32)
    entering = prefix(
        (decay_through[-1], state_through[-1]), "seq", chain_join, (ones_state, zeros_state)
    )[1]
    decay_before = jnp.concatenate([ones_state[None], decay_through[:-1]], axis=0)
    state_before = jnp.concatenate([zeros_state[None], state_through[:-1]], axis=0)
    block_starts = decay_before * entering[None] + state_before
    ssm_cols = recur_blocks(
        block_starts, step_cols, drive_cols, entry_cols, readout_cols, negative_rate
    )[1]
    ssm = ssm_cols.transpose(1, 0, 2).reshape(tokens, channels)
    mixed = (
        (ssm + skip_gain[None, :] * inner.astype(jnp.float32))
        * jax.nn.silu(gate_in.astype(jnp.float32))
    ).astype(jnp.bfloat16)
    rows = tokens // lax.axis_size("tp")
    mixer_sum = lax.psum_scatter(
        jnp.dot(mixed, out_weight, preferred_element_type=jnp.float32),
        "tp",
        scatter_dimension=0,
        tiled=True,
    )
    mixer_out = (mixer_sum + residual_in.astype(jnp.float32)).astype(jnp.bfloat16)
    mixer_wide = mixer_out.astype(jnp.float32)
    normed = (
        mixer_wide
        * lax.rsqrt(jnp.mean(mixer_wide * mixer_wide, axis=1, keepdims=True) + 1e-06)
        * norm_gain[None, :]
    ).astype(jnp.bfloat16)
    seq_count = lax.axis_size("seq")
    devices = seq_count * lax.axis_size("tp")
    seq_group = seq_count // EXPERTS
    capacity = 3 * rows // EXPERTS
    chosen = expert_ids.reshape(-1)
    expert_hits = (chosen[:, None] == jnp.arange(EXPERTS, dtype=jnp.int32)[None, :]).astype(
        jnp.int32
    )
    earlier_hits = jnp.cumsum(expert_hits, axis=0) - expert_hits
    slot_index = jnp.sum(earlier_hits * expert_hits, axis=1)
    target = chosen * capacity + slot_index
    placing = (jnp.arange(EXPERTS * capacity, dtype=jnp.int32)[:, None] == target[None, :]).astype(
        jnp.bfloat16
    )
    placing = jnp.sum(placing.reshape(EXPERTS * capacity, rows, 2), axis=2)
    slots_out = (
        jnp.dot(placing, normed, preferred_element_type=jnp.float32)
        .astype(jnp.bfloat16)
        .reshape(EXPERTS, capacity, width)
    )
    along_seq = jnp.repeat(slots_out, seq_group, axis=0)
    arrived_seq = lax.all_to_all(along_seq, "seq", split_axis=0, concat_axis=0, tiled=True)
    arrived_all = lax.all_gather(
        arrived_seq.reshape(1, seq_count * capacity, width), "tp", axis=0, tiled=True
    )
    arrived_flat = arrived_all.reshape(devices * capacity, width)
    summed = lax.psum_scatter(
        expert_share(arrived_flat, up_weight, down_weight).astype(jnp.float32).astype(jnp.bfloat16),
        "tp",
        scatter_dimension=0,
        tiled=True,
    ).astype(jnp.float32)
    home = lax.all_to_all(
        summed.reshape(seq_count, capacity, width).astype(jnp.bfloat16),
        "seq",
        split_axis=0,
        concat_axis=0,
        tiled=True,
    ).astype(jnp.float32)
    expert_out = jnp.sum(home.reshape(EXPERTS, seq_group, capacity, width), axis=1).reshape(
        EXPERTS * capacity, width
    )
    picked = jnp.take(expert_out, target, axis=0).reshape(rows, 2, width)
    layer_out = (mixer_wide + jnp.sum(picked * gate_prob[:, :, None], axis=1)).astype(jnp.bfloat16)
    return (mixer_out, layer_out)


def solution(mesh):
    return jax.shard_map(
        per_device,
        mesh=mesh,
        in_specs=(
            P("seq", "tp"),
            P("seq", "tp"),
            P(None, "tp"),
            P("tp"),
            P("tp", None),
            P(None, "tp"),
            P("tp"),
            P("tp", None),
            P("tp"),
            P("tp", None),
            P(("seq", "tp"), None),
            P(),
            P(("seq", "tp"), None),
            P(("seq", "tp"), None),
            P(None, ("seq", "tp")),
            P(("seq", "tp"), None),
        ),
        out_specs=(P(("seq", "tp"), None), P(("seq", "tp"), None)),
        check_vma=False,
    )
```

profile of v0, /device:TPU:0, one launch (start us, length us, event | category | flops | bytes accessed | tf_op | source)
XLA Modules:
  0.0 464.8 jit_solution(15491746981362353329)
XLA Ops:
  7.2 0.9 slice.130
  8.1 4.9 %collective-permute-start = (bf16[3,2048]{1,0:T(4,128)(2,1)S(1)}, bf16[3,2048]{1,0:T(4,128)(2,1)S(1)}, u32[]{:S(2)}, u32[]{:S(2)}) collective-permute-start(bf16[3,2048]{1,0:T(4,128)(2,1)S(1)} %slice.130), channel_id=1, source_target_pairs={{0,4},{4,8},{8,12},{12,16},{16,20},{20,24},{24,28},{1,5},{5,9},{9,... | collective-permute-start | bytes 36872 | tf_op jit(solution)/shard_map/ppermute | solution.py:14
  13.0 0.9 fusion.36
  14.5 1.2 maximum_convert_fusion
  15.7 1.4 multiply_convert_fusion.2
  17.9 1.5 fusion.39
  19.5 33.8 %all-reduce.16.cloned.1.call-done = f32[128,544]{0,1:T(8,128)} async-done(((f32[128,544]{0,1:T(8,128)}), f32[128,544]{0,1:T(8,128)}) %all-reduce.16.cloned.1.call-update) | async-done | bytes 278544 | tf_op jit(solution)/shard_map/psum | solution.py:88
  53.3 2.7 convert_multiply_fusion.2
  56.6 2.6 copy_bitcast_fusion
  59.1 1.3 fusion.34
  60.6 22.9 %while.37 = (s32[]{:T(128)}, f32[8,16,2048]{2,1,0:T(8,128)S(1)}, f32[16,8,2048]{2,1,0:T(8,128)}, f32[16,2048]{1,0:T(8,128)S(1)}, f32[16,8,16]{2,1,0:T(8,128)S(1)...) while((s32[]{:T(128)}, f32[8,16,2048]{2,1,0:T(8,128)S(1)}, f32[16,8,2048]{2,1,0:T(8,128)}, ...), condition=%wide.region_3.4_spmd.clone, body=%wide.region_2.3_spmd.clone.sunk | while | flops 1310723 | bytes 2623079 | solution.py:44
  60.7 0.9 dynamic-slice_bitcast_fusion.13
  62.1 0.9 dynamic-slice_bitcast_fusion.13
  63.5 0.9 dynamic-slice_bitcast_fusion.13
  64.9 0.9 dynamic-slice_bitcast_fusion.13
  66.4 0.9 dynamic-slice_bitcast_fusion.13
  67.8 0.9 dynamic-slice_bitcast_fusion.13
  69.2 0.9 dynamic-slice_bitcast_fusion.13
  70.7 0.9 dynamic-slice_bitcast_fusion.13
  76.4 0.9 dynamic-slice_bitcast_fusion.13
  80.7 0.9 dynamic-slice_bitcast_fusion.13
  87.4 2.4 pad.48
  89.9 2.4 pad.49
  92.3 2.1 add.214
  94.4 4.2 pad.102
  98.5 1.6 pad_maximum_fusion.2
  100.1 2.4 pad.42
  102.6 2.4 pad.43
  105.0 2.2 add_multiply_fusion.1
  107.3 2.4 pad.50
  109.7 1.6 slice_add_fusion.3
  111.4 1.3 add.207
  112.7 2.3 pad.104
  115.0 1.6 slice.276
  116.7 2.3 pad.45
  119.0 2.4 pad.67
  121.4 1.9 pad_maximum_fusion
  123.3 4.2 pad.44
  128.4 2.4 slice_add_fusion.5
  130.8 1.0 slice_add_fusion
  131.9 20.2 %all-gather.6.cloned.1.call-done = f32[8,16,2048]{2,1,0:T(8,128)} async-done(((f32[1,16,2048]{2,1,0:T(8,128)}), f32[8,16,2048]{2,1,0:T(8,128)}) %all-gather.6.cloned.1.call-update) | async-done | bytes 1048592 | tf_op jit(solution)/shard_map/all_gather | solution.py:19
  152.1 41.6 %all-gather.4.cloned.1.call-done = f32[8,16,2048]{2,1,0:T(8,128)} async-done(((f32[1,16,2048]{2,1,0:T(8,128)}), f32[8,16,2048]{2,1,0:T(8,128)}) %all-gather.4.cloned.1.call-update) | async-done | bytes 1048592 | tf_op jit(solution)/shard_map/all_gather | solution.py:19
  193.9 1.3 pad_add_fusion
  195.3 36.9 %while.36 = (s32[]{:T(128)}, f32[8,16,2048]{2,1,0:T(8,128)S(1)}, f32[16,8,2048]{2,1,0:T(8,128)}, f32[16,8,2048]{2,1,0:T(8,128)}, f32[16,2048]{1,0:T(8,128)S(1)},...) while((s32[]{:T(128)}, f32[8,16,2048]{2,1,0:T(8,128)S(1)}, ...), condition=%wide.region_8.9_spmd, body=%wide.region_6.8_spmd.sunk | while | flops 1556482 | bytes 2821733 | solution.py:44
  195.3 0.9 dynamic-slice_bitcast_fusion.12
  232.2 1.8 copy.55
  234.1 1.0 fusion.4
  235.1 9.5 %fusion.40 = f32[128,4096]{1,0:T(8,128)} fusion(bf16[128,2048]{1,0:T(8,128)(2,1)S(1)} %fusion.4, bf16[2048,4096]{1,0:T(8,128)(2,1)} %param.31), kind=kOutput, calls=%fused_computation.108 | convolution fusion | flops 2147483648 | bytes 19398656 | tf_op jit(solution)/shard_map/dot_general | solution.py:129
  245.6 36.9 %reduce-scatter.3.cloned.1.call-done = f32[32,4096]{1,0:T(8,128)} async-done(((f32[128,4096]{1,0:T(8,128)}), f32[32,4096]{1,0:T(8,128)}) %reduce-scatter.3.cloned.1.call-update) | async-done | bytes 524304 | tf_op jit(solution)/shard_map/reduce_scatter | solution.py:128
  282.4 1.2 fusion.12
  285.0 31.1 %all_to_all.10 = bf16[8,12,4096]{2,1,0:T(8,128)(2,1)S(1)} all-to-all(bf16[8,12,4096]{2,1,0:T(8,128)(2,1)S(1)} %reshape_broadcast_in_dim_reshape.3), channel_id=1, replica_groups=mesh['seq'=8,'tp'=4] {'seq'}, dimensions={0} | all-to-all | bytes 1572864 | tf_op jit(solution)/shard_map/all_to_all | solution.py:162
  316.1 1.1 reshape.138
  317.4 26.5 %all-gather.8.cloned.1.call-done = bf16[4,96,4096]{2,1,0:T(8,128)(2,1)} async-done(((bf16[1,96,4096]{2,1,0:T(8,128)(2,1)}), bf16[4,96,4096]{2,1,0:T(8,128)(2,1)}) %all-gather.8.cloned.1.call-update) | async-done | bytes 3145744 | tf_op jit(solution)/shard_map/all_gather | solution.py:163
  343.9 16.0 %multiply_convert_fusion.5 = bf16[384,3072]{1,0:T(8,128)(2,1)S(1)} fusion(bf16[384,4096]{1,0:T(8,128)(2,1)} %bitcast.97, bf16[4096,3072]{1,0:T(8,128)(2,1)} %param.36), kind=kOutput, calls=%fused_computation.16.clone.clone.1 | convolution fusion | flops 9669574656 | bytes 30670848 | tf_op jit(solution)/shard_map/dot_general | solution.py:53
  360.0 15.9 %convolution_convert_fusion = bf16[384,4096]{1,0:T(8,128)(2,1)} fusion(bf16[3072,4096]{1,0:T(8,128)(2,1)} %param.37, bf16[384,3072]{1,0:T(8,128)(2,1)S(1)} %multiply_convert_fusion.5), kind=kOutput, calls=%fused_computation.15 | convolution fusion | flops 9665249280 | bytes 30670848 | tf_op jit(solution)/shard_map/dot_general | solution.py:55
  375.9 38.1 %reduce-scatter.5.cloned.1.call-done = bf16[96,4096]{1,0:T(8,128)(2,1)} async-done(((bf16[384,4096]{1,0:T(8,128)(2,1)}), bf16[96,4096]{1,0:T(8,128)(2,1)}) %reduce-scatter.5.cloned.1.call-update) | async-done | bytes 786448 | tf_op jit(solution)/shard_map/reduce_scatter | solution.py:167
  414.0 2.2 convert_element_type.72
  416.2 5.5 %all-to-all-start.1 = ((bf16[8,12,4096]{2,1,0:T(8,128)(2,1)}), bf16[8,12,4096]{2,1,0:T(8,128)(2,1)S(1)}, u32[]{:S(2)}, u32[]{:S(2)}) async-start(bf16[8,12,4096]{2,1,0:T(8,128)(2,1)} %convert_element_type.72), calls=%async_computation.3 | async-start | bytes 2097152 | tf_op jit(solution)/shard_map/all_to_all | solution.py:173
  422.1 25.4 %all-to-all-done.1 = bf16[8,12,4096]{2,1,0:T(8,128)(2,1)S(1)} async-done(((bf16[8,12,4096]{2,1,0:T(8,128)(2,1)}), bf16[8,12,4096]{2,1,0:T(8,128)(2,1)S(1)}, u32[]{:S(2)}, u32[]{:S(2)}) %all-to-all-start.1) | async-done | bytes 786464 | tf_op jit(solution)/shard_map/all_to_all | solution.py:173
  447.5 1.4 reshape.143
  448.8 2.9 gather_fusion
  451.8 1.6 gather.7
  453.4 2.9 multiply_reduce_fusion.1
  456.3 1.7 fusion.15
  (198 shorter events, 59.3 us)
Async XLA Ops:
  7.2 10.8 %copy-start = (bf16[2048,544]{0,1:T(8,128)(2,1)S(1)}, bf16[2048,544]{0,1:T(8,128)(2,1)}, u32[]{:S(2)}) copy-start(bf16[2048,544]{0,1:T(8,128)(2,1)} %param.26) | copy-start | bytes 6684676
  7.2 46.1 %all-reduce.16.cloned.1.call-start = ((), (), s32[]{:S(2)}) async-start(), calls=%async_computation.4 | async-start | bytes 557056 | tf_op jit(solution)/shard_map/psum | solution.py:88
  8.1 6.3 %collective-permute-start = (bf16[3,2048]{1,0:T(4,128)(2,1)S(1)}, bf16[3,2048]{1,0:T(4,128)(2,1)S(1)}, u32[]{:S(2)}, u32[]{:S(2)}) collective-permute-start(bf16[3,2048]{1,0:T(4,128)(2,1)S(1)} %slice.130), channel_id=1, source_target_pairs={{0,4},{4,8},{8,12},{12,16},{16,20},{20,24},{24,28},{1,5},{5,9},{9,... | collective-permute-start | bytes 36872 | tf_op jit(solution)/shard_map/ppermute | solution.py:14
  14.0 3.1 copy-start.12
  14.0 3.1 copy-start.14
  15.6 3.8 copy-start.11
  15.7 37.6 %copy-start.19 = (f32[2048]{0:T(1024)S(1)}, f32[2048]{0:T(1024)}, u32[]{:S(2)}) copy-start(f32[2048]{0:T(1024)} %param.28) | copy-start | bytes 24580
  17.1 0.8 copy-start.2
  19.4 132.7 %all-gather.6.cloned.1.call-start = ((), (), s32[]{:S(2)}) async-start(), calls=%async_computation.6 | async-start | bytes 1179648 | tf_op jit(solution)/shard_map/all_gather | solution.py:19
  100.1 7.1 %copy-start.9 = (f32[1,16,2048]{2,1,0:T(8,128)S(1)}, f32[1,16,2048]{2,1,0:T(8,128)}, u32[]{:S(2)}) copy-start(f32[1,16,2048]{2,1,0:T(8,128)} %slice.154) | copy-start | bytes 393220
  111.4 82.4 %all-gather.4.cloned.1.call-start = ((), (), s32[]{:S(2)}) async-start(), calls=%async_computation.5 | async-start | bytes 1179648 | tf_op jit(solution)/shard_map/all_gather | solution.py:19
  116.6 165.9 %reduce-scatter.3.cloned.1.call-start = ((), (), s32[]{:S(2)}) async-start(), calls=%async_computation.7 | async-start | bytes 2621440 | tf_op jit(solution)/shard_map/reduce_scatter | solution.py:128
  116.7 11.8 %copy-start.3 = (f32[8,16,2048]{2,1,0:T(8,128)S(1)}, f32[8,16,2048]{2,1,0:T(8,128)}, u32[]{:S(2)}) copy-start(f32[8,16,2048]{2,1,0:T(8,128)} %pad.102) | copy-start | bytes 3145732
  121.4 9.4 %copy-start.4 = (f32[8,16,2048]{2,1,0:T(8,128)S(1)}, f32[8,16,2048]{2,1,0:T(8,128)}, u32[]{:S(2)}) copy-start(f32[8,16,2048]{2,1,0:T(8,128)} %pad.45) | copy-start | bytes 3145732
  128.4 2.4 copy-start.5
  130.8 63.1 %copy-start.6 = (f32[7,16,2048]{2,1,0:T(8,128)S(1)}, f32[7,16,2048]{2,1,0:T(8,128)}, u32[]{:S(2)}) copy-start(f32[7,16,2048]{2,1,0:T(8,128)} %slice_add_fusion.5) | copy-start | bytes 2752516
  195.3 38.8 %copy-start.8 = (bf16[128,2048]{1,0:T(8,128)(2,1)S(1)}, bf16[128,2048]{1,0:T(8,128)(2,1)}, u32[]{:S(2)}) copy-start(bf16[128,2048]{1,0:T(8,128)(2,1)} %param.23) | copy-start | bytes 1572868
  195.3 38.8 %copy-start.13 = (f32[1,2048]{1,0:T(1,128)S(1)}, f32[1,2048]{1,0:T(1,128)}, u32[]{:S(2)}) copy-start(f32[1,2048]{1,0:T(1,128)} %copy-done.12) | copy-start | bytes 24580
  195.3 38.8 %copy-start.15 = (f32[1,2048]{1,0:T(1,128)S(1)}, f32[1,2048]{1,0:T(1,128)}, u32[]{:S(2)}) copy-start(f32[1,2048]{1,0:T(1,128)} %copy-done.14) | copy-start | bytes 24580
  195.3 38.8 %copy-start.16 = (f32[2048]{0:T(1024)S(1)}, f32[2048]{0:T(1024)}, u32[]{:S(2)}) copy-start(f32[2048]{0:T(1024)} %param.25) | copy-start | bytes 24580
  195.3 38.8 %copy-start.20 = (f32[2048]{0:T(1024)S(1)}, f32[2048]{0:T(1024)}, u32[]{:S(2)}) copy-start(f32[2048]{0:T(1024)} %param.30) | copy-start | bytes 24580
  235.1 9.6 %copy-start.18 = (s32[32,2]{0,1:T(2,128)S(1)}, s32[32,2]{0,1:T(2,128)}, u32[]{:S(2)}) copy-start(s32[32,2]{0,1:T(2,128)} %param.34) | copy-start | bytes 772
  235.1 47.3 %copy-start.10 = (bf16[32,4096]{1,0:T(8,128)(2,1)S(1)}, bf16[32,4096]{1,0:T(8,128)(2,1)}, u32[]{:S(2)}) copy-start(bf16[32,4096]{1,0:T(8,128)(2,1)} %param.32) | copy-start | bytes 786436
  244.6 39.7 %copy-start.17 = (f32[4096]{0:T(1024)S(1)}, f32[4096]{0:T(1024)}, u32[]{:S(2)}) copy-start(f32[4096]{0:T(1024)} %param.33) | copy-start | bytes 49156
  244.7 99.3 %all-gather.8.cloned.1.call-start = ((), (), s32[]{:S(2)}) async-start(), calls=%async_computation.8 | async-start | bytes 3932160 | tf_op jit(solution)/shard_map/all_gather | solution.py:163
  283.7 0.7 copy-start.7
  317.2 96.8 %reduce-scatter.5.cloned.1.call-start = ((), (), s32[]{:S(2)}) async-start(), calls=%async_computation.9 | async-start | bytes 3932160 | tf_op jit(solution)/shard_map/reduce_scatter | solution.py:167
  375.9 46.1 %copy-start.21 = (f32[32,2]{0,1:T(2,128)S(1)}, f32[32,2]{0,1:T(2,128)}, u32[]{:S(2)}) copy-start(f32[32,2]{0,1:T(2,128)} %param.35) | copy-start | bytes 772
  416.2 31.3 %all-to-all-start.1 = ((bf16[8,12,4096]{2,1,0:T(8,128)(2,1)}), bf16[8,12,4096]{2,1,0:T(8,128)(2,1)S(1)}, u32[]{:S(2)}, u32[]{:S(2)}) async-start(bf16[8,12,4096]{2,1,0:T(8,128)(2,1)} %convert_element_type.72), calls=%async_computation.3 | async-start | bytes 2097152 | tf_op jit(solution)/shard_map/all_to_all | solution.py:173
  448.8 9.1 %copy-start.1 = (bf16[2048,544]{0,1:T(8,128)(2,1)S(1)}, bf16[2048,544]{0,1:T(8,128)(2,1)}, u32[]{:S(2)}) copy-start(bf16[2048,544]{0,1:T(8,128)(2,1)} %param.26) | copy-start | bytes 6684676
Sparse Core Ops, SparseCore 0:
  19.5 33.7 all-reduce.15
  111.5 40.5 all-gather.5
  154.8 38.8 all-gather.3
  244.8 37.5 reduce-scatter.2
  317.3 26.5 all-gather.7
  376.0 37.9 reduce-scatter.4
where the time goes:
time: 467 us; the launch traced here: 465 us
  waiting for transfers between devices  223 us (48%)
  local copies, waits for them, and re-layouts  88.8 us (19%)
  other arithmetic  49.3 us (11%)
  matrix products  46.1 us (10%)
  blocking collectives  31.1 us (7%)
  between operations  14.6 us (3%)
  starting transfers between devices  10.9 us (2%)
    all_gather x2, waiting for transfers between devices, prefix(): gathered = jax.tree.map(lambda a: lax.all_gather(a, axis), part)  61.9 us
    reduce_scatter x1, waiting for transfers between devices, per_device(): lax.psum_scatter(expert_share(arrived_flat, up_weight, down_weight).astyp...  38.1 us
    reduce_scatter x1, waiting for transfers between devices, per_device(): lax.psum_scatter(jnp.dot(mixed, out_weight, preferred_element_type=jnp.fl...  36.9 us
    psum x1, waiting for transfers between devices, per_device(): lax.psum(jnp.dot(inner, x_weight, preferred_element_type=jnp.float32), 'tp')  33.8 us
    all_to_all x1, blocking collectives, per_device(): lax.all_to_all(along_seq, 'seq', split_axis=0, concat_axis=0, tiled=True)  31.1 us
    mul x48, local copies, waits for them, and re-layouts, advance(): entry_row[:, :, None] * drive_row[:, None, :]  28.5 us
    all_gather x1, waiting for transfers between devices, per_device(): lax.all_gather(arrived_seq.reshape(1, seq_count * capacity, width), 'tp',...  26.5 us
    all_to_all x1, waiting for transfers between devices, per_device(): lax.all_to_all(summed.reshape(seq_count, capacity, width).astype(jnp.bflo...  25.4 us
  transfers between devices with their start and end apart: 8, of which 8 were waited for; matrix products, arithmetic and copies ran while one was open for 5% of the time, Pallas kernels for 0%

commit v1 on v0

--- a/solution.py
+++ b/solution.py
@@ -85,7 +85,9 @@
         )
     )
     inner = jax.nn.silu(conv_out).astype(jnp.bfloat16)
-    projected = lax.psum(jnp.dot(inner, x_weight, preferred_element_type=jnp.float32), "tp")
+    x = jnp.dot(inner, x_weight, preferred_element_type=jnp.float32)
+    parts = lax.all_gather(x, "tp", axis=0, tiled=False)
+    projected = parts.sum(axis=0)
     dt_low = projected[:, :DTRANK].astype(jnp.bfloat16)
     entry_rows = projected[:, DTRANK : DTRANK + STATE]
     readout_rows = projected[:, DTRANK + STATE :]

time: 467 us -> 457 us (0.979)
  waiting for transfers between devices: 223 us -> 208 us
    psum x1 -> x0, waiting for transfers between devices: 33.8 us -> none  [per_device(): lax.psum(jnp.dot(inner, x_weight, preferred_element_type=jnp.float32), 'tp')]
    all_gather x0 -> x1, waiting for transfers between devices: none -> 19.3 us  [per_device(): parts = lax.all_gather(x, 'tp', axis=0, tiled=False)]
where the time goes in v1:
time: 457 us; the launch traced here: 455 us
  waiting for transfers between devices  208 us (46%)
  local copies, waits for them, and re-layouts  92.6 us (20%)
  other arithmetic  50.2 us (11%)
  matrix products  46 us (10%)
  blocking collectives  31.1 us (7%)
  between operations  14.6 us (3%)
  starting transfers between devices  10.9 us (2%)
    all_gather x2, waiting for transfers between devices, prefix(): gathered = jax.tree.map(lambda a: lax.all_gather(a, axis), part)  61.4 us
    reduce_scatter x1, waiting for transfers between devices, per_device(): lax.psum_scatter(expert_share(arrived_flat, up_weight, down_weight).astyp...  38.1 us
    reduce_scatter x1, waiting for transfers between devices, per_device(): lax.psum_scatter(jnp.dot(mixed, out_weight, preferred_element_type=jnp.fl...  36.9 us
    all_to_all x1, blocking collectives, per_device(): lax.all_to_all(along_seq, 'seq', split_axis=0, concat_axis=0, tiled=True)  31.1 us
    mul x48, local copies, waits for them, and re-layouts, advance(): entry_row[:, :, None] * drive_row[:, None, :]  28.4 us
    all_gather x1, waiting for transfers between devices, per_device(): lax.all_gather(arrived_seq.reshape(1, seq_count * capacity, width), 'tp',...  26.5 us
    all_to_all x1, waiting for transfers between devices, per_device(): lax.all_to_all(summed.reshape(seq_count, capacity, width).astype(jnp.bflo...  25.4 us
    all_gather x1, waiting for transfers between devices, per_device(): parts = lax.all_gather(x, 'tp', axis=0, tiled=False)  19.3 us
  transfers between devices with their start and end apart: 8, of which 8 were waited for; matrix products, arithmetic and copies ran while one was open for 5% of the time, Pallas kernels for 0%

profile of v1, /device:TPU:0, one launch (start us, length us, event | category | flops | bytes accessed | tf_op | source)
XLA Modules:
  0.0 454.6 jit_solution(4166044561626022139)
XLA Ops:
  7.2 0.9 slice.130
  8.1 4.9 %collective-permute-start = (bf16[3,2048]{1,0:T(4,128)(2,1)S(1)}, bf16[3,2048]{1,0:T(4,128)(2,1)S(1)}, u32[]{:S(2)}, u32[]{:S(2)}) collective-permute-start(bf16[3,2048]{1,0:T(4,128)(2,1)S(1)} %slice.130), channel_id=1, source_target_pairs={{0,4},{4,8},{8,12},{12,16},{16,20},{20,24},{24,28},{1,5},{5,9},{9,... | collective-permute-start | bytes 36872 | tf_op jit(solution)/shard_map/ppermute | solution.py:14
  13.0 0.9 fusion.36
  14.5 1.2 maximum_convert_fusion
  15.6 1.4 multiply_convert_fusion.2
  17.8 1.5 fusion.39
  19.4 19.3 %all-gather.12.cloned.1.call-done = f32[512,544]{0,1:T(8,128)} async-done(((f32[128,544]{0,1:T(8,128)}), f32[512,544]{0,1:T(8,128)}) %all-gather.12.cloned.1.call-update) | async-done | bytes 1114128 | tf_op jit(solution)/shard_map/all_gather | solution.py:89
  38.7 2.6 reshape.152
  41.3 1.9 reduce_sum.74
  44.5 2.7 convert_multiply_fusion.2
  47.8 2.6 copy_bitcast_fusion
  50.6 22.9 %while.37 = (s32[]{:T(128)}, f32[8,16,2048]{2,1,0:T(8,128)S(1)}, f32[16,8,2048]{2,1,0:T(8,128)}, f32[16,2048]{1,0:T(8,128)S(1)}, f32[16,8,16]{2,1,0:T(8,128)S(1)...) while((s32[]{:T(128)}, f32[8,16,2048]{2,1,0:T(8,128)S(1)}, f32[16,8,2048]{2,1,0:T(8,128)}, ...), condition=%wide.region_3.4_spmd.clone, body=%wide.region_2.3_spmd.clone.sunk | while | flops 1310723 | bytes 2623079 | solution.py:44
  50.6 0.9 dynamic-slice_bitcast_fusion.13
  52.0 0.9 dynamic-slice_bitcast_fusion.13
  53.4 0.9 dynamic-slice_bitcast_fusion.13
  54.9 0.9 dynamic-slice_bitcast_fusion.13
  56.3 0.9 dynamic-slice_bitcast_fusion.13
  57.7 0.9 dynamic-slice_bitcast_fusion.13
  59.2 0.9 dynamic-slice_bitcast_fusion.13
  60.6 0.9 dynamic-slice_bitcast_fusion.13
  66.3 0.9 dynamic-slice_bitcast_fusion.13
  70.6 0.9 dynamic-slice_bitcast_fusion.13
  77.5 2.4 pad.48
  79.9 2.4 pad.49
  82.4 2.1 add.212
  84.4 4.2 pad.102
  88.6 1.6 pad_maximum_fusion.2
  90.2 2.4 pad.42
  92.6 2.4 pad.43
  95.1 2.3 add_multiply_fusion.1
  97.4 2.4 pad.50
  99.8 1.6 slice_add_fusion.3
  101.5 1.3 add.205
  102.8 2.3 pad.104
  105.1 1.6 slice.276
  106.8 2.5 pad.45
  109.3 4.1 pad.67
  114.3 4.1 pad.44
  118.6 2.3 slice_add_fusion.5
  121.0 1.0 slice_add_fusion
  122.0 19.8 %all-gather.8.cloned.1.call-done = f32[8,16,2048]{2,1,0:T(8,128)} async-done(((f32[1,16,2048]{2,1,0:T(8,128)}), f32[8,16,2048]{2,1,0:T(8,128)}) %all-gather.8.cloned.1.call-update) | async-done | bytes 1048592 | tf_op jit(solution)/shard_map/all_gather | solution.py:19
  141.8 41.6 %all-gather.6.cloned.1.call-done = f32[8,16,2048]{2,1,0:T(8,128)} async-done(((f32[1,16,2048]{2,1,0:T(8,128)}), f32[8,16,2048]{2,1,0:T(8,128)}) %all-gather.6.cloned.1.call-update) | async-done | bytes 1048592 | tf_op jit(solution)/shard_map/all_gather | solution.py:19
  183.7 1.3 pad_add_fusion
  185.0 37.0 %while.36 = (s32[]{:T(128)}, f32[8,16,2048]{2,1,0:T(8,128)S(1)}, f32[16,8,2048]{2,1,0:T(8,128)}, f32[16,8,2048]{2,1,0:T(8,128)}, f32[16,2048]{1,0:T(8,128)S(1)},...) while((s32[]{:T(128)}, f32[8,16,2048]{2,1,0:T(8,128)S(1)}, ...), condition=%wide.region_8.9_spmd, body=%wide.region_6.8_spmd.sunk | while | flops 1556482 | bytes 2821733 | solution.py:44
  185.0 0.9 dynamic-slice_bitcast_fusion.12
  222.0 1.9 copy.57
  224.0 1.0 fusion.4
  225.0 9.5 %fusion.40 = f32[128,4096]{1,0:T(8,128)} fusion(bf16[128,2048]{1,0:T(8,128)(2,1)S(1)} %fusion.4, bf16[2048,4096]{1,0:T(8,128)(2,1)} %param.31), kind=kOutput, calls=%fused_computation.108 | convolution fusion | flops 2147483648 | bytes 19398656 | tf_op jit(solution)/shard_map/dot_general | solution.py:131
  235.4 36.9 %reduce-scatter.3.cloned.1.call-done = f32[32,4096]{1,0:T(8,128)} async-done(((f32[128,4096]{1,0:T(8,128)}), f32[32,4096]{1,0:T(8,128)}) %reduce-scatter.3.cloned.1.call-update) | async-done | bytes 524304 | tf_op jit(solution)/shard_map/reduce_scatter | solution.py:130
  272.3 1.2 fusion.12
  274.8 31.1 %all_to_all.10 = bf16[8,12,4096]{2,1,0:T(8,128)(2,1)S(1)} all-to-all(bf16[8,12,4096]{2,1,0:T(8,128)(2,1)S(1)} %reshape_broadcast_in_dim_reshape.3), channel_id=1, replica_groups=mesh['seq'=8,'tp'=4] {'seq'}, dimensions={0} | all-to-all | bytes 1572864 | tf_op jit(solution)/shard_map/all_to_all | solution.py:164
  305.9 1.1 reshape.138
  307.3 26.5 %all-gather.10.cloned.1.call-done = bf16[4,96,4096]{2,1,0:T(8,128)(2,1)} async-done(((bf16[1,96,4096]{2,1,0:T(8,128)(2,1)}), bf16[4,96,4096]{2,1,0:T(8,128)(2,1)}) %all-gather.10.cloned.1.call-update) | async-done | bytes 3145744 | tf_op jit(solution)/shard_map/all_gather | solution.py:165
  333.8 16.0 %multiply_convert_fusion.5 = bf16[384,3072]{1,0:T(8,128)(2,1)S(1)} fusion(bf16[384,4096]{1,0:T(8,128)(2,1)} %bitcast.99, bf16[4096,3072]{1,0:T(8,128)(2,1)} %param.36), kind=kOutput, calls=%fused_computation.16.clone.clone.1 | convolution fusion | flops 9669574656 | bytes 30670848 | tf_op jit(solution)/shard_map/dot_general | solution.py:53
  349.8 15.9 %convolution_convert_fusion = bf16[384,4096]{1,0:T(8,128)(2,1)} fusion(bf16[3072,4096]{1,0:T(8,128)(2,1)} %param.37, bf16[384,3072]{1,0:T(8,128)(2,1)S(1)} %multiply_convert_fusion.5), kind=kOutput, calls=%fused_computation.15 | convolution fusion | flops 9665249280 | bytes 30670848 | tf_op jit(solution)/shard_map/dot_general | solution.py:55
  365.7 38.1 %reduce-scatter.5.cloned.1.call-done = bf16[96,4096]{1,0:T(8,128)(2,1)} async-done(((bf16[384,4096]{1,0:T(8,128)(2,1)}), bf16[96,4096]{1,0:T(8,128)(2,1)}) %reduce-scatter.5.cloned.1.call-update) | async-done | bytes 786448 | tf_op jit(solution)/shard_map/reduce_scatter | solution.py:169
  403.9 2.2 convert_element_type.72
  406.0 5.5 %all-to-all-start.1 = ((bf16[8,12,4096]{2,1,0:T(8,128)(2,1)}), bf16[8,12,4096]{2,1,0:T(8,128)(2,1)S(1)}, u32[]{:S(2)}, u32[]{:S(2)}) async-start(bf16[8,12,4096]{2,1,0:T(8,128)(2,1)} %convert_element_type.72), calls=%async_computation.3 | async-start | bytes 2097152 | tf_op jit(solution)/shard_map/all_to_all | solution.py:175
  412.0 25.4 %all-to-all-done.1 = bf16[8,12,4096]{2,1,0:T(8,128)(2,1)S(1)} async-done(((bf16[8,12,4096]{2,1,0:T(8,128)(2,1)}), bf16[8,12,4096]{2,1,0:T(8,128)(2,1)S(1)}, u32[]{:S(2)}, u32[]{:S(2)}) %all-to-all-start.1) | async-done | bytes 786464 | tf_op jit(solution)/shard_map/all_to_all | solution.py:175
  437.3 1.4 reshape.143
  438.7 2.9 gather_fusion
  441.6 1.6 gather.7
  443.2 2.9 multiply_reduce_fusion.1
  446.1 1.7 fusion.15
  (211 shorter events, 60.9 us)
Async XLA Ops:
  7.2 10.7 %copy-start = (bf16[2048,544]{0,1:T(8,128)(2,1)S(1)}, bf16[2048,544]{0,1:T(8,128)(2,1)}, u32[]{:S(2)}) copy-start(bf16[2048,544]{0,1:T(8,128)(2,1)} %param.26) | copy-start | bytes 6684676
  7.2 31.5 %all-gather.12.cloned.1.call-start = ((), (), s32[]{:S(2)}) async-start(), calls=%async_computation.9 | async-start | bytes 1392640 | tf_op jit(solution)/shard_map/all_gather | solution.py:89
  8.1 6.3 %collective-permute-start = (bf16[3,2048]{1,0:T(4,128)(2,1)S(1)}, bf16[3,2048]{1,0:T(4,128)(2,1)S(1)}, u32[]{:S(2)}, u32[]{:S(2)}) collective-permute-start(bf16[3,2048]{1,0:T(4,128)(2,1)S(1)} %slice.130), channel_id=1, source_target_pairs={{0,4},{4,8},{8,12},{12,16},{16,20},{20,24},{24,28},{1,5},{5,9},{9,... | collective-permute-start | bytes 36872 | tf_op jit(solution)/shard_map/ppermute | solution.py:14
  14.0 3.0 copy-start.16
  14.0 3.0 copy-start.18
  17.0 0.8 copy-start.3
  17.8 1.5 copy-start.15
  19.3 25.2 %copy-start.24 = (f32[2048]{0:T(1024)S(1)}, f32[2048]{0:T(1024)}, u32[]{:S(2)}) copy-start(f32[2048]{0:T(1024)} %param.28) | copy-start | bytes 24580
  19.3 122.5 %all-gather.8.cloned.1.call-start = ((), (), s32[]{:S(2)}) async-start(), calls=%async_computation.5 | async-start | bytes 1179648 | tf_op jit(solution)/shard_map/all_gather | solution.py:19
  43.2 0.7 copy-start.11
  73.6 33.2 %copy-start.2 = (f32[8,16,2048]{2,1,0:T(8,128)}, f32[8,16,2048]{2,1,0:T(8,128)S(1)}, u32[]{:S(2)}) copy-start(f32[8,16,2048]{2,1,0:T(8,128)S(1)} %multiply_exponential_fusion) | copy-start | bytes 3145732
  90.2 7.1 %copy-start.13 = (f32[1,16,2048]{2,1,0:T(8,128)S(1)}, f32[1,16,2048]{2,1,0:T(8,128)}, u32[]{:S(2)}) copy-start(f32[1,16,2048]{2,1,0:T(8,128)} %slice.154) | copy-start | bytes 393220
  97.4 4.1 copy-start.4
  101.5 81.9 %all-gather.6.cloned.1.call-start = ((), (), s32[]{:S(2)}) async-start(), calls=%async_computation.4 | async-start | bytes 1179648 | tf_op jit(solution)/shard_map/all_gather | solution.py:19
  102.8 10.7 %copy-start.10 = (f32[3,16,2048]{2,1,0:T(8,128)S(1)}, f32[3,16,2048]{2,1,0:T(8,128)}, u32[]{:S(2)}) copy-start(f32[3,16,2048]{2,1,0:T(8,128)} %get-tuple-element.250) | copy-start | bytes 1179652
  106.7 165.5 %reduce-scatter.3.cloned.1.call-start = ((), (), s32[]{:S(2)}) async-start(), calls=%async_computation.6 | async-start | bytes 2621440 | tf_op jit(solution)/shard_map/reduce_scatter | solution.py:130
  106.8 6.6 %slice-start = ((f32[8,16,2048]{2,1,0:T(8,128)}), f32[1,16,2048]{2,1,0:T(8,128)S(1)}, s32[]{:S(2)}) async-start(f32[8,16,2048]{2,1,0:T(8,128)} %copy-done.2), calls=%async_computation.10 | async-start | bytes 262144 | tf_op jit(solution)/shard_map/slice | solution.py:110
  109.3 9.1 %copy-start.21 = (f32[128,16]{0,1:T(8,128)S(1)}, f32[128,16]{0,1:T(8,128)}, u32[]{:S(2)}) copy-start(f32[128,16]{0,1:T(8,128)} %get-tuple-element.260) | copy-start | bytes 24580
  109.3 9.3 %copy-start.5 = (f32[8,16,2048]{2,1,0:T(8,128)S(1)}, f32[8,16,2048]{2,1,0:T(8,128)}, u32[]{:S(2)}) copy-start(f32[8,16,2048]{2,1,0:T(8,128)} %pad.102) | copy-start | bytes 3145732
  114.3 6.7 %copy-start.6 = (f32[8,16,2048]{2,1,0:T(8,128)S(1)}, f32[8,16,2048]{2,1,0:T(8,128)}, u32[]{:S(2)}) copy-start(f32[8,16,2048]{2,1,0:T(8,128)} %pad.45) | copy-start | bytes 3145732
  118.6 2.4 copy-start.7
  121.0 62.7 %copy-start.8 = (f32[7,16,2048]{2,1,0:T(8,128)S(1)}, f32[7,16,2048]{2,1,0:T(8,128)}, u32[]{:S(2)}) copy-start(f32[7,16,2048]{2,1,0:T(8,128)} %slice_add_fusion.5) | copy-start | bytes 2752516
  185.0 39.0 %copy-start.17 = (f32[1,2048]{1,0:T(1,128)S(1)}, f32[1,2048]{1,0:T(1,128)}, u32[]{:S(2)}) copy-start(f32[1,2048]{1,0:T(1,128)} %copy-done.16) | copy-start | bytes 24580
  185.0 39.0 %copy-start.19 = (f32[1,2048]{1,0:T(1,128)S(1)}, f32[1,2048]{1,0:T(1,128)}, u32[]{:S(2)}) copy-start(f32[1,2048]{1,0:T(1,128)} %copy-done.18) | copy-start | bytes 24580
  185.0 39.0 %copy-start.20 = (f32[2048]{0:T(1024)S(1)}, f32[2048]{0:T(1024)}, u32[]{:S(2)}) copy-start(f32[2048]{0:T(1024)} %param.25) | copy-start | bytes 24580
  185.0 39.0 %copy-start.25 = (f32[2048]{0:T(1024)S(1)}, f32[2048]{0:T(1024)}, u32[]{:S(2)}) copy-start(f32[2048]{0:T(1024)} %param.30) | copy-start | bytes 24580
  222.0 1.9 copy-start.12
  225.0 9.6 %copy-start.23 = (s32[32,2]{0,1:T(2,128)S(1)}, s32[32,2]{0,1:T(2,128)}, u32[]{:S(2)}) copy-start(s32[32,2]{0,1:T(2,128)} %param.34) | copy-start | bytes 772
  234.5 37.8 %copy-start.14 = (bf16[32,4096]{1,0:T(8,128)(2,1)S(1)}, bf16[32,4096]{1,0:T(8,128)(2,1)}, u32[]{:S(2)}) copy-start(bf16[32,4096]{1,0:T(8,128)(2,1)} %param.32) | copy-start | bytes 786436
  234.5 39.8 %copy-start.22 = (f32[4096]{0:T(1024)S(1)}, f32[4096]{0:T(1024)}, u32[]{:S(2)}) copy-start(f32[4096]{0:T(1024)} %param.33) | copy-start | bytes 49156
  234.5 99.3 %all-gather.10.cloned.1.call-start = ((), (), s32[]{:S(2)}) async-start(), calls=%async_computation.7 | async-start | bytes 3932160 | tf_op jit(solution)/shard_map/all_gather | solution.py:165
  273.5 0.7 copy-start.9
  307.0 96.9 %reduce-scatter.5.cloned.1.call-start = ((), (), s32[]{:S(2)}) async-start(), calls=%async_computation.8 | async-start | bytes 3932160 | tf_op jit(solution)/shard_map/reduce_scatter | solution.py:169
  365.7 46.1 %copy-start.26 = (f32[32,2]{0,1:T(2,128)S(1)}, f32[32,2]{0,1:T(2,128)}, u32[]{:S(2)}) copy-start(f32[32,2]{0,1:T(2,128)} %param.35) | copy-start | bytes 772
  406.0 31.3 %all-to-all-start.1 = ((bf16[8,12,4096]{2,1,0:T(8,128)(2,1)}), bf16[8,12,4096]{2,1,0:T(8,128)(2,1)S(1)}, u32[]{:S(2)}, u32[]{:S(2)}) async-start(bf16[8,12,4096]{2,1,0:T(8,128)(2,1)} %convert_element_type.72), calls=%async_computation.3 | async-start | bytes 2097152 | tf_op jit(solution)/shard_map/all_to_all | solution.py:175
  438.7 9.1 %copy-start.1 = (bf16[2048,544]{0,1:T(8,128)(2,1)S(1)}, bf16[2048,544]{0,1:T(8,128)(2,1)}, u32[]{:S(2)}) copy-start(bf16[2048,544]{0,1:T(8,128)(2,1)} %param.26) | copy-start | bytes 6684676
Sparse Core Ops, SparseCore 0:
  19.5 19.2 all-gather.11
  101.6 40.1 all-gather.7
  144.5 38.8 all-gather.5
  234.6 37.6 reduce-scatter.2
  307.1 26.5 all-gather.9
  365.9 37.9 reduce-scatter.4
